TPU v7x, 32 devices: a whole 2x2x4 slice. The times are simulated.
32 devices in a mesh: dom: 32 (over z, y, x, core).
Axes of the slice: x: 2, y: 2, z: 4, core: 2. Of those that a mesh axis runs over, the one named last changes fastest.
Arguments:
- coef_init: float32 [1024, 128], P('dom'), may hold values from -6 to 6
- basis: bfloat16 [49152, 1024], P('dom'), may hold values from -0.375 to 0.375
- basis_scale: float32 [384], P('dom'), may hold values from 0.5 to 2
- ext_force: float32 [49152, 128], P('dom'), may hold values from -6 to 6
- precond: float32 [1024], P('dom'), may hold values from 0.5 to 6, as said below
- connectivity: int32 [14400, 8], P('dom'), may hold values from 0 to 767, as said below
- halo_nodes: int32 [8192], P('dom'), may hold values from 0 to 511, as said below
- plastic: int32 [14400], P('dom'), may hold values 0 or 1
Outputs:
- coef_final: float32 [1024, 128], P('dom')
- nodal_residual: float32 [49152, 128], P('dom')
Inputs may be any that keep to these rules, and one draw needn't show every extreme that they name: `connectivity`: each part is a structured block of 16 x 16 x 2 nodes, numbered in a part-specific order; each row lists an element's 8 corners in corner-bit order (bit 0 along x, bit 1 along y, bit 2 along z). Entries below 512 are the part's own nodes; an entry 512 + h names the node listed h-th in the next part's halo_nodes (the next part's first z layer). `halo_nodes`: the entries of one part are its own local node numbers of its first z layer, in grid order with x fastest, all distinct. `precond`: Positive.
All inputs are finite; a program needn't handle non-finite values. No bound on the sum of `plastic` on one device may be relied on, other than what follows from the above.
Results may differ from a plain program's by a relative error of at most 0.0087.
Values may be sent and summed in bfloat16 or wider, within the bound.
No kernel may reach another device: no remote copies, remote signals or barrier semaphores. Data moves between devices by JAX's collectives and lax.ppermute only.
A program may use at most 64 MiB of HBM per device.

v0:
```python
import jax
import jax.numpy as jnp
from jax import lax
from jax.sharding import PartitionSpec as P

R = 1024
ITERS = 2
STEP_SIZE = 0.5
SHEAR_MODULUS = 1.0
LAME_FIRST = 1.5
HARDENING = 0.5
YIELD_STRESS = 3.0
EPSILON = 1e-05


def from_behind(value, axis, steps):
    count = lax.axis_size(axis)
    leading, last = (max(0, -steps), min(count, count - steps))
    return lax.ppermute(value, axis, [(source, source + steps) for source in range(leading, last)])


def corner_table():
    corner_bits = jnp.arange(8)[:, None] >> jnp.arange(3)[None, :] & 1
    return (2.0 * corner_bits.astype(jnp.float32) - 1.0) / 4.0


def element_forces(corner_disp, flags, corners):
    gradient = jnp.einsum("eaic,aj->eijc", corner_disp, corners, precision=lax.Precision.HIGHEST)
    strain = 0.5 * (gradient + jnp.swapaxes(gradient, 1, 2))
    volumetric = strain[:, 0, 0] + strain[:, 1, 1] + strain[:, 2, 2]
    identity = jnp.eye(3, dtype=jnp.float32)[None, :, :, None]
    shear_part = 2.0 * SHEAR_MODULUS * (strain - volumetric[:, None, None] / 3.0 * identity)
    magnitude = jnp.sqrt(jnp.sum(shear_part * shear_part, axis=(1, 2)))
    total_modulus = 2.0 * SHEAR_MODULUS + HARDENING
    plastic_factor = HARDENING / total_modulus + 2.0 * SHEAR_MODULUS * YIELD_STRESS / (
        total_modulus * jnp.maximum(magnitude, YIELD_STRESS)
    )
    factor = jnp.where(flags[:, None] == 1, plastic_factor, jnp.ones_like(plastic_factor))
    stress = LAME_FIRST * volumetric[:, None, None] * identity + factor[:, None, None] * shear_part
    return jnp.einsum("eijc,aj->eaic", stress, corners, precision=lax.Precision.HIGHEST)


def apply_scale(values, scales):
    return (values.reshape(scales.shape[0], -1, values.shape[-1]) * scales[:, None, None]).reshape(
        values.shape
    )


def on_device(coef_init, basis, basis_scale, ext_force, precond, connectivity, halo_nodes, plastic):
    rows_dev, cases = ext_force.shape
    node_count = rows_dev // 3
    halo_count = halo_nodes.shape[0]
    owned_rows = coef_init.shape[0]
    corners = corner_table()
    node_ids = jnp.arange(node_count + halo_count, dtype=jnp.int32)
    incidence = (node_ids[:, None] == connectivity.reshape(-1)[None, :]).astype(jnp.float32)
    nodal_residual = ext_force
    coef_full, precond_full = (
        lax.all_gather(coef_init, "dom", axis=0, tiled=True),
        lax.all_gather(precond, "dom", axis=0, tiled=True),
    )
    for sweep in range(ITERS):
        lifted = jnp.dot(basis, coef_full.astype(jnp.bfloat16), preferred_element_type=jnp.float32)
        nodes = apply_scale(lifted, basis_scale).reshape(node_count, 3, cases)
        outgoing = nodes[halo_nodes]
        incoming = from_behind(outgoing, "dom", -1)
        extended = jnp.concatenate([nodes, incoming], axis=0)
        corner_force = element_forces(extended[connectivity], plastic, corners)
        internal = jnp.dot(
            incidence,
            corner_force.reshape(-1, 3 * cases),
            precision=lax.Precision.HIGHEST,
            preferred_element_type=jnp.float32,
        ).reshape(node_count + halo_count, 3, cases)
        returned = from_behind(internal[node_count:], "dom", 1)
        own_force = internal[:node_count].at[halo_nodes].add(returned)
        nodal_residual = ext_force - own_force.reshape(rows_dev, cases)
        scaled = apply_scale(nodal_residual, basis_scale).astype(jnp.bfloat16)
        partial_sum = lax.dot_general(
            basis, scaled, (((0,), (0,)), ((), ())), preferred_element_type=jnp.float32
        )
        reduced = lax.psum(partial_sum, "dom")
        update = precond_full[:, None] * reduced
        root_mean = jnp.sqrt(jnp.sum(update * update, axis=0) / R + EPSILON)
        coef_full = coef_full + STEP_SIZE * update / root_mean
    coef_out = lax.dynamic_slice_in_dim(
        coef_full, lax.axis_index("dom") * owned_rows, owned_rows, 0
    )
    return (coef_out, nodal_residual)


def solution(mesh):
    return jax.shard_map(
        on_device,
        mesh=mesh,
        in_specs=(
            P("dom", None),
            P("dom", None),
            P("dom"),
            P("dom", None),
            P("dom"),
            P("dom", None),
            P("dom"),
            P("dom"),
        ),
        out_specs=(P("dom", None), P("dom", None)),
        check_vma=False,
    )
```

profile of v0, /device:TPU:0, one launch (start us, length us, event | category | flops | bytes accessed | tf_op | source)
XLA Modules:
  0.0 553.9 jit_solution(8672493367761439965)
XLA Ops:
  7.2 45.1 %all_gather.6 = f32[1024,128]{1,0:T(8,128)S(1)} all-gather(f32[32,128]{1,0:T(8,128)} %param.8), channel_id=1, replica_groups=mesh['dom'=32] {'dom'}, dimensions={0}, use_global_device_ids=true | all-gather | bytes 540672 | tf_op jit(solution)/shard_map/all_gather | solution.py:59
  53.1 1.9 fusion.15
  55.0 2.3 reshape.100
  57.7 2.8 broadcast_multiply_fusion.1
  60.5 3.0 gather_fusion
  63.5 1.3 collective-permute-start
  68.7 3.0 pad_maximum_fusion
  71.6 14.1 %gather_fusion.1 = f32[3600,3,128]{2,1,0:T(4,128)} fusion(f32[768,3,128]{2,1,0:T(4,128)} %pad_maximum_fusion, s32[4096]{0:T(1024)S(1)} %pad_clamp_fusion), kind=kCustom, calls=%fused_computation.1 | custom fusion | bytes 11073600 | tf_op jit(solution)/shard_map/gather | solution.py:68
  85.8 8.2 %fusion.6 = f32[3,450,3,128]{3,0,2,1:T(4,128)S(1)} fusion(f32[450,8,3,128]{3,2,1,0:T(4,128)} %bitcast.78), kind=kOutput, calls=%fused_computation.15 | convolution fusion | flops 49766544 | bytes 7603200 | tf_op jit(solution)/shard_map/eaic,aj->eijc/dot_general | solution.py:28
  95.9 2.2 multiply_reduce_fusion.1
  98.3 4.6 multiply_add_fusion.1
  102.9 6.6 %convolution_bitcast_fusion.1 = f32[3600,384]{1,0:T(8,128)S(1)} fusion(f32[450,3,3,128]{3,1,2,0:T(4,128)S(1)} %multiply_add_fusion.1), kind=kOutput, calls=%fused_computation.10 | convolution fusion | flops 49766544 | bytes 7603200 | tf_op jit(solution)/shard_map/eijc,aj->eaic/dot_general | solution.py:40
  109.5 8.3 %fusion.1 = f32[768,384]{0,1:T(8,128)S(1)} fusion(f32[3600,384]{1,0:T(8,128)S(1)} %convolution_bitcast_fusion.1, s32[3600]{0:T(1024)S(1)} %eq.35), kind=kOutput, calls=%fused_computation.8 | convolution fusion | flops 12742963200 | bytes 6723648 | tf_op jit(solution)/shard_map/dot_general | solution.py:69
  119.6 2.0 copy.42
  121.6 8.7 %collective-permute-start.1 = (f32[256,3,128]{2,1,0:T(4,128)}, f32[256,3,128]{2,1,0:T(4,128)}, u32[]{:S(2)}, u32[]{:S(2)}) collective-permute-start(f32[256,3,128]{2,1,0:T(4,128)} %copy.42), channel_id=1, source_target_pairs={{0,1},{1,2},{2,3},{3,4},{4,5},{5,6},{6,7},{7,8},{8,9},{9,10},{10,1... | collective-permute-start | bytes 1179656 | tf_op jit(solution)/shard_map/ppermute | solution.py:19
  130.3 2.1 slice.67
  132.4 2.5 copy.43
  134.8 26.6 %scatter_fusion = f32[512,3,128]{2,1,0:T(4,128)} fusion(f32[512,3,128]{2,1,0:T(4,128)} %copy.43, s32[256]{0:T(256)S(1)} %compare_select_fusion.1, f32[256,3,128]{2,1,0:T(4,128)} %collective-permute-done.1), kind=kCustom, calls=%fused_computation.4 | custom fusion | flops 98304 | bytes 1180672 | tf_op jit(solution)/shard_map/scatter-add | solution.py:76
  161.4 2.3 reshape.102
  163.7 3.2 convolution_bitcast_fusion.4
  166.9 2.0 copy.44
  169.2 38.4 %all-reduce = f32[1024]{0:T(1024)S(1)} all-reduce(f32[1024]{0:T(1024)S(1)} %dynamic-update-slice), channel_id=1, replica_groups=mesh['dom'=32] {'dom'}, use_global_device_ids=true, to_apply=%add | all-reduce | flops 1024 | bytes 8192
  207.6 87.8 %all-reduce.4.cloned.1.call-done = f32[1024,128]{0,1:T(8,128)} async-done(((f32[1024,128]{0,1:T(8,128)}), f32[1024,128]{0,1:T(8,128)}) %all-reduce.4.cloned.1.call-update) | async-done | bytes 524304 | tf_op jit(solution)/shard_map/psum | solution.py:82
  295.3 1.2 multiply_reduce_fusion.3
  296.5 1.3 divide_add_fusion
  298.7 2.1 convolution_bitcast_fusion.2
  300.7 2.3 copy.45
  303.1 2.3 reshape.103
  305.4 2.8 broadcast_multiply_fusion
  308.2 3.0 gather_fusion.2
  311.2 1.3 collective-permute-start.2
  312.5 2.7 collective-permute-done.2
  315.2 2.8 pad_maximum_fusion.1
  318.0 14.1 %gather_fusion.3 = f32[3600,3,128]{2,1,0:T(4,128)} fusion(f32[768,3,128]{2,1,0:T(4,128)} %pad_maximum_fusion.1, s32[4096]{0:T(1024)S(1)} %pad_clamp_fusion), kind=kCustom, calls=%fused_computation.3 | custom fusion | bytes 11073600 | tf_op jit(solution)/shard_map/gather | solution.py:68
  332.2 8.2 %fusion.4 = f32[3,450,3,128]{3,0,2,1:T(4,128)S(1)} fusion(f32[450,8,3,128]{3,2,1,0:T(4,128)} %bitcast.77), kind=kOutput, calls=%fused_computation.13 | convolution fusion | flops 49766544 | bytes 7603200 | tf_op jit(solution)/shard_map/eaic,aj->eijc/dot_general | solution.py:28
  342.3 2.3 multiply_reduce_fusion
  344.7 4.6 multiply_add_fusion
  349.3 6.6 %convolution_bitcast_fusion = f32[3600,384]{1,0:T(8,128)S(1)} fusion(f32[450,3,3,128]{3,1,2,0:T(4,128)S(1)} %multiply_add_fusion), kind=kOutput, calls=%fused_computation.9 | convolution fusion | flops 49766544 | bytes 7603200 | tf_op jit(solution)/shard_map/eijc,aj->eaic/dot_general | solution.py:40
  355.9 8.3 %fusion = f32[768,384]{0,1:T(8,128)S(1)} fusion(f32[3600,384]{1,0:T(8,128)S(1)} %convolution_bitcast_fusion, s32[3600]{0:T(1024)S(1)} %eq.35), kind=kOutput, calls=%fused_computation.7 | convolution fusion | flops 12742963200 | bytes 6723648 | tf_op jit(solution)/shard_map/dot_general | solution.py:69
  366.3 9.3 %collective-permute-start.3 = (f32[256,3,128]{2,1,0:T(4,128)}, f32[256,3,128]{2,1,0:T(4,128)}, u32[]{:S(2)}, u32[]{:S(2)}) collective-permute-start(f32[256,3,128]{2,1,0:T(4,128)} %copy.50), channel_id=1, source_target_pairs={{0,1},{1,2},{2,3},{3,4},{4,5},{5,6},{6,7},{7,8},{8,9},{9,10},{10,1... | collective-permute-start | bytes 1179656 | tf_op jit(solution)/shard_map/ppermute | solution.py:19
  375.5 2.1 slice.72
  377.6 2.5 copy.51
  380.0 26.4 %scatter_fusion.1 = f32[512,3,128]{2,1,0:T(4,128)} fusion(f32[512,3,128]{2,1,0:T(4,128)} %copy.51, s32[256]{0:T(256)S(1)} %compare_select_fusion.1, f32[256,3,128]{2,1,0:T(4,128)} %collective-permute-done.3), kind=kCustom, calls=%fused_computation.5 | custom fusion | flops 98304 | bytes 1180672 | tf_op jit(solution)/shard_map/scatter-add | solution.py:76
  406.4 2.3 reshape.105
  408.7 1.5 sub.25
  411.0 1.8 convolution_bitcast_fusion.3
  412.8 131.2 %all-reduce.6.cloned.1.call-done = f32[1024,128]{0,1:T(8,128)} async-done(((f32[1024,128]{0,1:T(8,128)}), f32[1024,128]{0,1:T(8,128)}) %all-reduce.6.cloned.1.call-update) | async-done | bytes 524304 | tf_op jit(solution)/shard_map/psum | solution.py:82
  544.0 1.2 multiply_reduce_fusion.2
  (62 shorter events, 16.7 us)
Async XLA Ops:
  7.2 46.0 %copy-start = (bf16[1536,1024]{1,0:T(8,128)(2,1)S(1)}, bf16[1536,1024]{1,0:T(8,128)(2,1)}, u32[]{:S(2)}) copy-start(bf16[1536,1024]{1,0:T(8,128)(2,1)} %param.9) | copy-start | bytes 9437188
  7.2 288.1 %all-reduce.4.cloned.1.call-start = ((), (), s32[]{:S(2)}) async-start(), calls=%async_computation | async-start | bytes 1048576 | tf_op jit(solution)/shard_map/psum | solution.py:82
  52.3 0.8 copy-start.1
  53.1 4.2 copy-start.7
  53.1 4.5 copy-start.9
  55.0 9.8 %copy-start.6 = (s32[450,8]{0,1:T(8,128)S(1)}, s32[450,8]{0,1:T(8,128)}, u32[]{:S(2)}) copy-start(s32[450,8]{0,1:T(8,128)} %param.13) | copy-start | bytes 43204
  57.3 11.3 %copy-start.8 = (s32[450]{0:T(512)S(1)}, s32[450]{0:T(512)}, u32[]{:S(2)}) copy-start(s32[450]{0:T(512)} %param.15) | copy-start | bytes 5404
  63.5 5.2 collective-permute-start
  117.8 1.0 copy-start.4
  121.6 13.3 %collective-permute-start.1 = (f32[256,3,128]{2,1,0:T(4,128)}, f32[256,3,128]{2,1,0:T(4,128)}, u32[]{:S(2)}, u32[]{:S(2)}) collective-permute-start(f32[256,3,128]{2,1,0:T(4,128)} %copy.42), channel_id=1, source_target_pairs={{0,1},{1,2},{2,3},{3,4},{4,5},{5,6},{6,7},{7,8},{8,9},{9,10},{10,1... | collective-permute-start | bytes 1179656 | tf_op jit(solution)/shard_map/ppermute | solution.py:19
  163.7 5.3 copy-start.10
  166.9 377.2 %all-reduce.6.cloned.1.call-start = ((), (), s32[]{:S(2)}) async-start(), calls=%async_computation.1 | async-start | bytes 1048576 | tf_op jit(solution)/shard_map/psum | solution.py:82
  297.8 0.8 copy-start.3
  311.2 4.0 collective-permute-start.2
  364.2 1.0 copy-start.5
  366.3 13.8 %collective-permute-start.3 = (f32[256,3,128]{2,1,0:T(4,128)}, f32[256,3,128]{2,1,0:T(4,128)}, u32[]{:S(2)}, u32[]{:S(2)}) collective-permute-start(f32[256,3,128]{2,1,0:T(4,128)} %copy.50), channel_id=1, source_target_pairs={{0,1},{1,2},{2,3},{3,4},{4,5},{5,6},{6,7},{7,8},{8,9},{9,10},{10,1... | collective-permute-start | bytes 1179656 | tf_op jit(solution)/shard_map/ppermute | solution.py:19
  410.1 0.9 copy-start.2
Sparse Core Ops, SparseCore 0:
  167.0 128.2 all-reduce.3
  413.0 131.0 all-reduce.5
where the time goes:
time: 564 us; the launch traced here: 554 us
  waiting for transfers between devices  222 us (39%)
  other arithmetic  88.2 us (16%)
  blocking collectives  83.5 us (15%)
  local copies, waits for them, and re-layouts  70.3 us (12%)
  matrix products  55.1 us (10%)
  starting transfers between devices  20.6 us (4%)
  between operations  14.6 us (3%)
    psum x2, waiting for transfers between devices, on_device(): reduced = lax.psum(partial_sum, 'dom')  219 us
    scatter-add x2, other arithmetic, on_device(): own_force = internal[:node_count].at[halo_nodes].add(returned)  52.9 us
    all_gather x1, blocking collectives, on_device(): lax.all_gather(coef_init, 'dom', axis=0, tiled=True)  45.1 us
    unnamed x1, blocking collectives  38.4 us
    gather x2, local copies, waits for them, and re-layouts, on_device(): corner_force = element_forces(extended[connectivity], plastic, corners)  28.3 us
    ppermute x4, starting transfers between devices, from_behind(): lax.ppermute(value, axis, [(source, source + steps) for source in range(l...  20.5 us
    dot_general x2, matrix products, on_device(): jnp.dot(incidence, corner_force.reshape(-1, 3 * cases), precision=lax.Pre...  16.7 us
    dot_general x2, matrix products, element_forces(): jnp.einsum('eaic,aj->eijc', corner_disp, corners, precision=lax.Precision...  16.4 us
  transfers between devices with their start and end apart: 6, of which 3 were waited for; matrix products, arithmetic and copies ran while one was open for 3% of the time, Pallas kernels for 0%

commit v1 on v0

--- a/solution.py
+++ b/solution.py
@@ -79,7 +79,11 @@
         partial_sum = lax.dot_general(
             basis, scaled, (((0,), (0,)), ((), ())), preferred_element_type=jnp.float32
         )
-        reduced = lax.psum(partial_sum, "dom")
+
+        def unite_column(array_here):
+            return jnp.sum(lax.all_gather(array_here, "dom"), axis=0)
+
+        reduced = unite_column(partial_sum)
         update = precond_full[:, None] * reduced
         root_mean = jnp.sqrt(jnp.sum(update * update, axis=0) / R + EPSILON)
         coef_full = coef_full + STEP_SIZE * update / root_mean

time: 564 us -> 593 us (1.051)
  local copies, waits for them, and re-layouts: 70.3 us -> 106 us
  waiting for transfers between devices: 222 us -> 191 us
  other arithmetic: 88.2 us -> 109 us
    psum x2 -> x0, waiting for transfers between devices: 219 us -> none  [on_device(): reduced = lax.psum(partial_sum, 'dom')]
    all_gather x0 -> x2, waiting for transfers between devices: none -> 189 us  [unite_column(): return jnp.sum(lax.all_gather(array_here, 'dom'), axis=0)]
    unnamed x29, local copies, waits for them, and re-layouts: 6.35 us -> 41.6 us
    reduce_sum x0 -> x2, other arithmetic: none -> 19.6 us  [unite_column(): return jnp.sum(lax.all_gather(array_here, 'dom'), axis=0)]
where the time goes in v1:
time: 593 us; the launch traced here: 582 us
  waiting for transfers between devices  191 us (32%)
  other arithmetic  109 us (18%)
  local copies, waits for them, and re-layouts  106 us (18%)
  blocking collectives  85.4 us (14%)
  matrix products  55.3 us (9%)
  starting transfers between devices  21 us (4%)
  between operations  14.6 us (2%)
    all_gather x2, waiting for transfers between devices, unite_column(): return jnp.sum(lax.all_gather(array_here, 'dom'), axis=0)  189 us
    scatter-add x2, other arithmetic, on_device(): own_force = internal[:node_count].at[halo_nodes].add(returned)  53.1 us
    all_gather x1, blocking collectives, on_device(): lax.all_gather(coef_init, 'dom', axis=0, tiled=True)  44.9 us
    unnamed x29, local copies, waits for them, and re-layouts  41.6 us
    unnamed x1, blocking collectives  40.5 us
    gather x2, local copies, waits for them, and re-layouts, on_device(): corner_force = element_forces(extended[connectivity], plastic, corners)  28 us
    ppermute x4, starting transfers between devices, from_behind(): lax.ppermute(value, axis, [(source, source + steps) for source in range(l...  20.9 us
    reduce_sum x2, other arithmetic, unite_column(): return jnp.sum(lax.all_gather(array_here, 'dom'), axis=0)  19.6 us
  transfers between devices with their start and end apart: 6, of which 3 were waited for; matrix products, arithmetic and copies ran while one was open for 3% of the time, Pallas kernels for 0%

profile of v1, /device:TPU:0, one launch (start us, length us, event | category | flops | bytes accessed | tf_op | source)
XLA Modules:
  0.0 582.5 jit_solution(891808664279036132)
XLA Ops:
  9.1 44.9 %all_gather.18 = f32[1024,128]{1,0:T(8,128)S(1)} all-gather(f32[32,128]{1,0:T(8,128)} %param.8), channel_id=1, replica_groups=mesh['dom'=32] {'dom'}, dimensions={0}, use_global_device_ids=true | all-gather | bytes 540672 | tf_op jit(solution)/shard_map/all_gather | solution.py:59
  54.8 1.9 fusion.15
  56.7 2.3 reshape.100
  59.0 2.8 broadcast_multiply_fusion.1
  61.8 3.0 gather_fusion
  70.0 3.0 pad_maximum_fusion
  73.0 13.9 %gather_fusion.1 = f32[3600,3,128]{2,1,0:T(4,128)} fusion(f32[768,3,128]{2,1,0:T(4,128)} %pad_maximum_fusion, s32[4096]{0:T(1024)S(1)} %pad_clamp_fusion), kind=kCustom, calls=%fused_computation.1 | custom fusion | bytes 11073600 | tf_op jit(solution)/shard_map/gather | solution.py:68
  86.8 8.2 %fusion.6 = f32[3,450,3,128]{3,0,2,1:T(4,128)S(1)} fusion(f32[450,8,3,128]{3,2,1,0:T(4,128)} %bitcast.88), kind=kOutput, calls=%fused_computation.17 | convolution fusion | flops 49766544 | bytes 7603200 | tf_op jit(solution)/shard_map/eaic,aj->eijc/dot_general | solution.py:28
  97.0 2.2 multiply_reduce_fusion.1
  99.4 4.6 multiply_add_fusion.1
  103.9 6.8 %convolution_bitcast_fusion.1 = f32[3600,384]{1,0:T(8,128)S(1)} fusion(f32[450,3,3,128]{3,1,2,0:T(4,128)S(1)} %multiply_add_fusion.1), kind=kOutput, calls=%fused_computation.12 | convolution fusion | flops 49766544 | bytes 7603200 | tf_op jit(solution)/shard_map/eijc,aj->eaic/dot_general | solution.py:40
  110.8 8.3 %fusion.1 = f32[768,384]{0,1:T(8,128)S(1)} fusion(f32[3600,384]{1,0:T(8,128)S(1)} %convolution_bitcast_fusion.1, s32[3600]{0:T(1024)S(1)} %eq.35), kind=kOutput, calls=%fused_computation.10 | convolution fusion | flops 12742963200 | bytes 6723648 | tf_op jit(solution)/shard_map/dot_general | solution.py:69
  120.9 2.0 copy.55
  122.9 8.7 %collective-permute-start.1 = (f32[256,3,128]{2,1,0:T(4,128)}, f32[256,3,128]{2,1,0:T(4,128)}, u32[]{:S(2)}, u32[]{:S(2)}) collective-permute-start(f32[256,3,128]{2,1,0:T(4,128)} %copy.55), channel_id=1, source_target_pairs={{0,1},{1,2},{2,3},{3,4},{4,5},{5,6},{6,7},{7,8},{8,9},{9,10},{10,1... | collective-permute-start | bytes 1179656 | tf_op jit(solution)/shard_map/ppermute | solution.py:19
  131.6 2.1 slice.67
  133.7 2.5 copy.56
  136.1 26.5 %scatter_fusion = f32[512,3,128]{2,1,0:T(4,128)} fusion(f32[512,3,128]{2,1,0:T(4,128)} %copy.56, s32[256]{0:T(256)S(1)} %compare_select_fusion.1, f32[256,3,128]{2,1,0:T(4,128)} %collective-permute-done.1), kind=kCustom, calls=%fused_computation.4 | custom fusion | flops 98304 | bytes 1180672 | tf_op jit(solution)/shard_map/scatter-add | solution.py:76
  162.7 2.3 reshape.102
  164.9 3.2 convolution_bitcast_fusion.4
  168.2 2.0 copy.57
  170.4 40.5 %all-reduce = f32[1024]{0:T(1024)S(1)} all-reduce(f32[1024]{0:T(1024)S(1)} %dynamic-update-slice), channel_id=1, replica_groups=mesh['dom'=32] {'dom'}, use_global_device_ids=true, to_apply=%add | all-reduce | flops 1024 | bytes 8192
  210.9 71.3 %all-gather.5.cloned.1.call-done = f32[32768,128]{0,1:T(8,128)} async-done(((f32[1024,128]{0,1:T(8,128)}), f32[32768,128]{0,1:T(8,128)}) %all-gather.5.cloned.1.call-update) | async-done | bytes 16777232 | tf_op jit(solution)/shard_map/all_gather | solution.py:84
  282.2 17.7 %copy.75 = f32[16,8,32,1024]{3,2,1,0:T(8,128)} copy(f32[16,8,32,1024]{3,1,2,0:T(8,128)} %bitcast.89) | data formatting | bytes 33554432
  299.9 9.8 %bitcast_reduce_fusion.1 = f32[1024,128]{0,1:T(8,128)} fusion(f32[16,8,32,1024]{3,2,1,0:T(8,128)} %copy.75), kind=kLoop, calls=%fused_computation.7 | loop fusion | flops 4063232 | bytes 17301504 | tf_op jit(solution)/shard_map/reduce_sum | solution.py:84
  310.9 1.3 divide_add_fusion
  313.0 2.1 convolution_bitcast_fusion.2
  315.1 2.3 copy.58
  317.4 2.3 reshape.103
  319.7 2.8 broadcast_multiply_fusion
  322.5 3.0 gather_fusion.2
  326.8 2.7 collective-permute-done.2
  329.5 2.8 pad_maximum_fusion.1
  332.3 14.1 %gather_fusion.3 = f32[3600,3,128]{2,1,0:T(4,128)} fusion(f32[768,3,128]{2,1,0:T(4,128)} %pad_maximum_fusion.1, s32[4096]{0:T(1024)S(1)} %pad_clamp_fusion), kind=kCustom, calls=%fused_computation.3 | custom fusion | bytes 11073600 | tf_op jit(solution)/shard_map/gather | solution.py:68
  346.4 8.2 %fusion.4 = f32[3,450,3,128]{3,0,2,1:T(4,128)S(1)} fusion(f32[450,8,3,128]{3,2,1,0:T(4,128)} %bitcast.87), kind=kOutput, calls=%fused_computation.15 | convolution fusion | flops 49766544 | bytes 7603200 | tf_op jit(solution)/shard_map/eaic,aj->eijc/dot_general | solution.py:28
  356.6 2.2 multiply_reduce_fusion
  359.0 4.6 multiply_add_fusion
  363.5 6.6 %convolution_bitcast_fusion = f32[3600,384]{1,0:T(8,128)S(1)} fusion(f32[450,3,3,128]{3,1,2,0:T(4,128)S(1)} %multiply_add_fusion), kind=kOutput, calls=%fused_computation.11 | convolution fusion | flops 49766544 | bytes 7603200 | tf_op jit(solution)/shard_map/eijc,aj->eaic/dot_general | solution.py:40
  370.1 8.3 %fusion = f32[768,384]{0,1:T(8,128)S(1)} fusion(f32[3600,384]{1,0:T(8,128)S(1)} %convolution_bitcast_fusion, s32[3600]{0:T(1024)S(1)} %eq.35), kind=kOutput, calls=%fused_computation.9 | convolution fusion | flops 12742963200 | bytes 6723648 | tf_op jit(solution)/shard_map/dot_general | solution.py:69
  380.5 9.7 %collective-permute-start.3 = (f32[256,3,128]{2,1,0:T(4,128)}, f32[256,3,128]{2,1,0:T(4,128)}, u32[]{:S(2)}, u32[]{:S(2)}) collective-permute-start(f32[256,3,128]{2,1,0:T(4,128)} %copy.63), channel_id=1, source_target_pairs={{0,1},{1,2},{2,3},{3,4},{4,5},{5,6},{6,7},{7,8},{8,9},{9,10},{10,1... | collective-permute-start | bytes 1179656 | tf_op jit(solution)/shard_map/ppermute | solution.py:19
  390.1 2.1 slice.72
  392.2 2.5 copy.64
  394.7 26.6 %scatter_fusion.1 = f32[512,3,128]{2,1,0:T(4,128)} fusion(f32[512,3,128]{2,1,0:T(4,128)} %copy.64, s32[256]{0:T(256)S(1)} %compare_select_fusion.1, f32[256,3,128]{2,1,0:T(4,128)} %collective-permute-done.3), kind=kCustom, calls=%fused_computation.5 | custom fusion | flops 98304 | bytes 1180672 | tf_op jit(solution)/shard_map/scatter-add | solution.py:76
  421.2 2.3 reshape.105
  423.5 1.5 sub.25
  425.8 1.8 convolution_bitcast_fusion.3
  427.7 117.4 %all-gather.7.cloned.1.call-done = f32[32768,128]{0,1:T(8,128)} async-done(((f32[1024,128]{0,1:T(8,128)}), f32[32768,128]{0,1:T(8,128)}) %all-gather.7.cloned.1.call-update) | async-done | bytes 16777232 | tf_op jit(solution)/shard_map/all_gather | solution.py:84
  545.1 17.7 %copy.76 = f32[16,8,32,1024]{3,2,1,0:T(8,128)} copy(f32[16,8,32,1024]{3,1,2,0:T(8,128)} %bitcast.90) | data formatting | bytes 33554432
  562.8 9.8 %bitcast_reduce_fusion = f32[1024,128]{0,1:T(8,128)} fusion(f32[16,8,32,1024]{3,2,1,0:T(8,128)} %copy.76), kind=kLoop, calls=%fused_computation.6 | loop fusion | flops 4063232 | bytes 17301504 | tf_op jit(solution)/shard_map/reduce_sum | solution.py:84
  (64 shorter events, 23.0 us)
Async XLA Ops:
  7.2 47.6 %copy-start = (bf16[1536,1024]{1,0:T(8,128)(2,1)S(1)}, bf16[1536,1024]{1,0:T(8,128)(2,1)}, u32[]{:S(2)}) copy-start(bf16[1536,1024]{1,0:T(8,128)(2,1)} %param.9) | copy-start | bytes 9437188
  7.2 275.0 %all-gather.5.cloned.1.call-start = ((), (), s32[]{:S(2)}) async-start(), calls=%async_computation | async-start | bytes 17301504 | tf_op jit(solution)/shard_map/all_gather | solution.py:84
  54.0 0.8 copy-start.1
  56.7 9.4 %copy-start.6 = (s32[450,8]{0,1:T(8,128)S(1)}, s32[450,8]{0,1:T(8,128)}, u32[]{:S(2)}) copy-start(s32[450,8]{0,1:T(8,128)} %param.13) | copy-start | bytes 43204
  56.7 13.3 %copy-start.8 = (s32[450]{0:T(512)S(1)}, s32[450]{0:T(512)}, u32[]{:S(2)}) copy-start(s32[450]{0:T(512)} %param.15) | copy-start | bytes 5404
  64.8 5.2 collective-permute-start
  110.7 20.8 %copy-start.7 = (f32[12]{0:T(128)S(1)}, f32[12]{0:T(128)}, u32[]{:S(2)}) copy-start(f32[12]{0:T(128)} %param.10) | copy-start | bytes 148
  119.1 1.0 copy-start.4
  122.9 13.3 %collective-permute-start.1 = (f32[256,3,128]{2,1,0:T(4,128)}, f32[256,3,128]{2,1,0:T(4,128)}, u32[]{:S(2)}, u32[]{:S(2)}) collective-permute-start(f32[256,3,128]{2,1,0:T(4,128)} %copy.55), channel_id=1, source_target_pairs={{0,1},{1,2},{2,3},{3,4},{4,5},{5,6},{6,7},{7,8},{8,9},{9,10},{10,1... | collective-permute-start | bytes 1179656 | tf_op jit(solution)/shard_map/ppermute | solution.py:19
  164.9 5.3 copy-start.9
  168.2 377.0 %all-gather.7.cloned.1.call-start = ((), (), s32[]{:S(2)}) async-start(), calls=%async_computation.1 | async-start | bytes 17301504 | tf_op jit(solution)/shard_map/all_gather | solution.py:84
  312.2 0.8 copy-start.3
  325.5 4.0 collective-permute-start.2
  378.5 1.0 copy-start.5
  380.5 14.2 %collective-permute-start.3 = (f32[256,3,128]{2,1,0:T(4,128)}, f32[256,3,128]{2,1,0:T(4,128)}, u32[]{:S(2)}, u32[]{:S(2)}) collective-permute-start(f32[256,3,128]{2,1,0:T(4,128)} %copy.63), channel_id=1, source_target_pairs={{0,1},{1,2},{2,3},{3,4},{4,5},{5,6},{6,7},{7,8},{8,9},{9,10},{10,1... | collective-permute-start | bytes 1179656 | tf_op jit(solution)/shard_map/ppermute | solution.py:19
  425.0 0.9 copy-start.2
Sparse Core Ops, SparseCore 0:
  168.3 113.8 all-gather.4
  427.8 117.2 all-gather.6
